TPU v7x, 256 devices: a whole 4x4x8 slice. The times are simulated.
256 devices in a mesh: view: 8 (over y, x_lo), band: 32 (over x_hi, z, core).
Axes of the slice: x: 4 (x_hi: 2, x_lo: 2; x = x_hi * 2 + x_lo), y: 4, z: 8, core: 2. Of those that a mesh axis runs over, the one named last changes fastest.
Arguments:
- features: float32 [8, 256, 512, 128], P('view', 'band'), may hold values from -6 to 6
- tempers: float32 [8, 256, 512], P('view', 'band'), may hold values from 0.5 to 80
- partners: int32 [8, 2], replicated, may hold values from 0 to 7, as said below
- conv_one: bfloat16 [3, 3, 128, 128], replicated, may hold values from -0.1875 to 0.1875
- conv_two: bfloat16 [3, 3, 128, 128], replicated, may hold values from -0.1875 to 0.1875
- query_weight: bfloat16 [128, 128], replicated, may hold values from -0.5 to 0.5
- key_weight: bfloat16 [128, 128], replicated, may hold values from -0.5 to 0.5
- value_weight: bfloat16 [128, 128], replicated, may hold values from -0.5 to 0.5
- out_weight: bfloat16 [128, 128], replicated, may hold values from -0.5 to 0.5
- norm_gain: float32 [128], replicated, may hold values from 0.25 to 1.75
- message_gain: float32 [128], replicated, may hold values from 0.25 to 1.75
Outputs:
- refined: float32 [8, 256, 512, 128], P('view', 'band')
Inputs may be any that keep to these rules, and one draw needn't show every extreme that they name: Column 0 and column 1 are each a permutation of the 8 views; a view is never its own partner, and its two partners differ. At least one view has as its first partner the view 4 positions away from it (modulo 8).
All inputs are finite; a program needn't handle non-finite values.
Results may differ from a plain program's by a relative error of at most 0.0065.
Values may be sent and summed in bfloat16 or wider, within the bound.
A program may use at most 64 MiB of HBM per device.

v0:
```python
import math
import jax
import jax.numpy as jnp
from jax import lax
from jax.sharding import PartitionSpec as P

epsilon = 1e-06


def extended(cells, sides, width):
    for axis, dim in sides:
        count = lax.axis_size(axis)
        ends = count - 1
        head = lax.slice_in_dim(cells, 0, width, axis=dim)
        tail = lax.slice_in_dim(cells, cells.shape[dim] - width, cells.shape[dim], axis=dim)
        cells = jnp.concatenate(
            [
                lax.ppermute(tail, axis, [(i, (i + 1) % count) for i in range(ends)]),
                cells,
                lax.ppermute(head, axis, [((i + 1) % count, i) for i in range(ends)]),
            ],
            axis=dim,
        )
    return cells


def root_norm(values, gain):
    mean_square = jnp.mean(values * values, axis=-1, keepdims=True)
    return values * lax.rsqrt(mean_square + epsilon) * gain


def convolve(padded, kernel):
    leading = padded.shape[:-3]
    out_rows = padded.shape[-3] - 2
    columns = padded.shape[-2]
    channels = padded.shape[-1]
    widened = jnp.pad(padded, [(0, 0)] * len(leading) + [(0, 0), (1, 1), (0, 0)])
    summed = jnp.zeros(leading + (out_rows, columns, kernel.shape[-1]), jnp.float32)
    for row_tap in range(3):
        for col_tap in range(3):
            window = widened[..., row_tap : row_tap + out_rows, col_tap : col_tap + columns, :]
            product = jnp.dot(
                window.reshape(-1, channels),
                kernel[row_tap, col_tap],
                preferred_element_type=jnp.float32,
            )
            summed = summed + product.reshape(summed.shape)
    return summed


def route_pair(normed_rows, own_view, partners):
    every_view = lax.all_gather(normed_rows[None], "view", axis=0, tiled=True)
    chosen = lax.dynamic_index_in_dim(partners, own_view, 0, keepdims=False)
    return jnp.take(every_view, chosen, axis=0)


def per_device(
    features,
    tempers,
    partners,
    conv_one,
    conv_two,
    query_weight,
    key_weight,
    value_weight,
    out_weight,
    norm_gain,
    message_gain,
):
    current = features[0]
    temper = tempers[0]
    row_count, columns, channels = current.shape
    first_input = jax.nn.silu(current).astype(jnp.bfloat16)
    first_rows = extended(first_input, (("band", 0),), 1)
    state_one = current + convolve(first_rows, conv_one)
    second_input = jax.nn.silu(state_one).astype(jnp.bfloat16)
    second_rows = extended(second_input, (("band", 0),), 1)
    state_two = state_one + convolve(second_rows, conv_two)
    normed = root_norm(state_two, norm_gain).astype(jnp.bfloat16)
    flat_normed = normed.reshape(-1, channels)
    queries = (
        jnp.dot(flat_normed, query_weight, preferred_element_type=jnp.float32)
        .astype(jnp.bfloat16)
        .reshape(normed.shape)
    )
    own_view = lax.axis_index("view")
    paired = route_pair(normed, own_view, partners)
    paired_rows = extended(paired, (("band", 1),), 1)
    pair_flat = paired_rows.reshape(-1, channels)
    key_rows = (
        jnp.dot(pair_flat, key_weight, preferred_element_type=jnp.float32)
        .astype(jnp.bfloat16)
        .reshape(paired_rows.shape)
    )
    value_rows = (
        jnp.dot(pair_flat, value_weight, preferred_element_type=jnp.float32)
        .astype(jnp.bfloat16)
        .reshape(paired_rows.shape)
    )
    block_size = min(columns, 512)
    factor = 1.0 / math.sqrt(channels)

    def attend_row(row_index):
        query_row = lax.dynamic_index_in_dim(queries, row_index, 0, keepdims=False)
        temper_row = lax.dynamic_index_in_dim(temper, row_index, 0, keepdims=False) * factor
        key_window = lax.dynamic_slice_in_dim(key_rows, row_index, 3, 1).reshape(
            2, 3 * columns, channels
        )
        value_window = lax.dynamic_slice_in_dim(value_rows, row_index, 3, 1).reshape(
            2, 3 * columns, channels
        )
        summed = jnp.zeros((columns, channels), jnp.float32)
        for partner in range(2):
            scores = lax.dot_general(
                query_row,
                key_window[partner],
                (((1,), (1,)), ((), ())),
                preferred_element_type=jnp.float32,
            )
            scores = scores * temper_row[0:block_size, None]
            row_peak = jnp.max(scores, axis=-1, keepdims=True)
            lifted = jnp.exp(scores - row_peak)
            shares = (lifted / jnp.sum(lifted, axis=-1, keepdims=True)).astype(jnp.bfloat16)
            pieces = [
                jnp.dot(shares, value_window[partner], preferred_element_type=jnp.float32).astype(
                    jnp.bfloat16
                )
            ]
            blended = jnp.concatenate(pieces, axis=0)
            summed = summed + jnp.dot(blended, out_weight, preferred_element_type=jnp.float32)
        return summed

    messages = lax.map(attend_row, jnp.arange(row_count, dtype=jnp.int32))
    refined = state_two + root_norm(messages, message_gain)
    return refined[None]


def solution(mesh):
    in_specs = (
        P("view", "band", None, None),
        P("view", "band", None),
        P(),
        P(),
        P(),
        P(),
        P(),
        P(),
        P(),
        P(),
        P(),
    )
    out_specs = P("view", "band", None, None)
    return jax.shard_map(
        per_device, mesh=mesh, in_specs=in_specs, out_specs=out_specs, check_vma=False
    )
```

profile of v0, /device:TPU:6, one launch (start us, length us, event | category | flops | bytes accessed | tf_op | source)
XLA Modules:
  0.0 379.8 jit_solution(6802062921291044743)
XLA Ops:
  6.5 2.3 fusion.19
  8.9 1.9 collective-permute-start
  10.8 8.0 %collective-permute-start.1 = (bf16[1,512,128]{2,1,0:T(8,128)(2,1)S(1)}, bf16[1,512,128]{2,1,0:T(8,128)(2,1)S(1)}, u32[]{:S(2)}, u32[]{:S(2)}) collective-permute-start(bf16[1,512,128]{2,1,0:T(8,128)(2,1)S(1)} %get-tuple-element.79), channel_id=1, source_target_pairs={{1,0},{2,1},{3,2},{4,3},{5,4},{6,5},{7,6},{8,7},{9,8},{10,9},{11,1... | collective-permute-start | bytes 393224 | tf_op jit(solution)/shard_map/ppermute | solution.py:20
  19.6 1.8 collective-permute-done.1
  26.2 1.9 collective-permute-start.2
  28.2 7.4 %collective-permute-start.3 = (bf16[1,512,128]{2,1,0:T(8,128)(2,1)S(1)}, bf16[1,512,128]{2,1,0:T(8,128)(2,1)S(1)}, u32[]{:S(2)}, u32[]{:S(2)}) collective-permute-start(bf16[1,512,128]{2,1,0:T(8,128)(2,1)S(1)} %get-tuple-element.77), channel_id=1, source_target_pairs={{1,0},{2,1},{3,2},{4,3},{5,4},{6,5},{7,6},{8,7},{9,8},{10,9},{11,1... | collective-permute-start | bytes 393224 | tf_op jit(solution)/shard_map/ppermute | solution.py:20
  36.3 1.8 collective-permute-done.3
  45.8 169.9 %all-gather.3.cloned.1.call-done = bf16[64,512,128]{2,1,0:T(8,128)(2,1)} async-done(((bf16[8,512,128]{2,1,0:T(8,128)(2,1)}), bf16[64,512,128]{2,1,0:T(8,128)(2,1)}) %all-gather.3.cloned.1.call-update) | async-done | bytes 8388624 | tf_op jit(solution)/shard_map/all_gather | solution.py:52
  215.7 4.3 %gather_fusion = bf16[2,8,512,128]{3,2,1,0:T(8,128)(2,1)S(1)} fusion(bf16[8,8,512,128]{3,2,1,0:T(8,128)(2,1)} %bitcast.194, s32[1024]{0:T(1024)S(1)} %pad_clamp_fusion), kind=kCustom, calls=%fused_computation | custom fusion | bytes 4194312 | tf_op jit(solution)/shard_map/jit(_take)/gather | solution.py:54
  220.4 1.9 collective-permute-start.4
  222.3 7.4 %collective-permute-start.5 = (bf16[2,1,512,128]{3,2,1,0:T(8,128)(2,1)S(1)}, bf16[2,1,512,128]{3,2,1,0:T(8,128)(2,1)S(1)}, u32[]{:S(2)}, u32[]{:S(2)}) collective-permute-start(bf16[2,1,512,128]{3,2,1,0:T(8,128)(2,1)S(1)} %get-tuple-element.75), channel_id=1, source_target_pairs={{1,0},{2,1},{3,2},{4,3},{5,4},{6,5},{7,6},{8,7},{9,8},{10,9},{11,1... | collective-permute-start | bytes 786440 | tf_op jit(solution)/shard_map/ppermute | solution.py:20
  231.7 1.8 collective-permute-done.5
  233.8 2.3 convolution_convert_fusion
  236.1 2.3 convolution_convert_fusion.1
  238.5 129.1 %while.10 = (s32[]{:T(128)}, f32[8,512,128]{2,1,0:T(8,128)}, s32[8]{0:T(128)S(1)}, bf16[8,512,128]{2,1,0:T(8,128)(2,1)}, bf16[2,10,512,128]{3,2,1,0:T(8,128)(2,1...) while((s32[]{:T(128)}, f32[8,512,128]{2,1,0:T(8,128)}, ...), condition=%wide.region_6.7_spmd, body=%wide.region_1.0_spmd.sunk | while | flops 850065920 | bytes 26308876 | solution.py:133
  242.5 2.4 constant_dynamic-slice_fusion.5
  244.9 1.6 fusion.146
  247.0 2.6 fusion.148
  252.1 2.5 fusion.151
  258.7 2.4 constant_dynamic-slice_fusion.5
  261.0 1.6 fusion.146
  263.2 2.6 fusion.148
  268.3 2.5 fusion.151
  274.8 2.4 constant_dynamic-slice_fusion.5
  277.2 1.6 fusion.146
  279.3 2.5 fusion.148
  284.4 2.5 fusion.151
  291.0 2.4 constant_dynamic-slice_fusion.5
  293.3 1.6 fusion.146
  295.5 2.6 fusion.148
  298.0 1.6 fusion.149
  300.6 2.5 fusion.151
  307.1 2.4 constant_dynamic-slice_fusion.5
  309.5 1.6 fusion.146
  311.6 2.6 fusion.148
  316.7 2.5 fusion.151
  323.2 2.4 constant_dynamic-slice_fusion.5
  325.6 1.6 fusion.146
  327.7 2.6 fusion.148
  332.9 2.5 fusion.151
  339.4 2.4 constant_dynamic-slice_fusion.5
  343.9 2.6 fusion.148
  349.0 2.5 fusion.151
  355.5 2.4 constant_dynamic-slice_fusion.5
  360.0 2.6 fusion.148
  365.1 2.5 fusion.151
  367.6 2.4 multiply_reduce_fusion
  370.0 2.9 add_bitcast_fusion
  (123 shorter events, 53.4 us)
Async XLA Ops:
  6.5 227.2 %copy-start = (bf16[128,128]{1,0:T(8,128)(2,1)S(1)}, bf16[128,128]{1,0:T(8,128)(2,1)}, u32[]{:S(2)}) copy-start(bf16[128,128]{1,0:T(8,128)(2,1)} %param.20) | copy-start | bytes 98308
  6.5 12.3 %copy-start.6 = (f32[1,8,512,128]{3,2,1,0:T(8,128)S(1)}, f32[1,8,512,128]{3,2,1,0:T(8,128)}, u32[]{:S(2)}) copy-start(f32[1,8,512,128]{3,2,1,0:T(8,128)} %param.13) | copy-start | bytes 6291460
  6.5 12.3 %copy-start.8 = (bf16[3,3,128,128]{3,2,1,0:T(8,128)(2,1)S(1)}, bf16[3,3,128,128]{3,2,1,0:T(8,128)(2,1)}, u32[]{:S(2)}) copy-start(bf16[3,3,128,128]{3,2,1,0:T(8,128)(2,1)} %param.16) | copy-start | bytes 884740
  6.5 209.2 %all-gather.3.cloned.1.call-start = ((), (), s32[]{:S(2)}) async-start(), calls=%async_computation | async-start | bytes 9437184 | tf_op jit(solution)/shard_map/all_gather | solution.py:52
  8.9 10.7 %collective-permute-start = (bf16[1,512,128]{2,1,0:T(8,128)(2,1)S(1)}, bf16[1,512,128]{2,1,0:T(8,128)(2,1)S(1)}, u32[]{:S(2)}, u32[]{:S(2)}) collective-permute-start(bf16[1,512,128]{2,1,0:T(8,128)(2,1)S(1)} %get-tuple-element.78), channel_id=1, source_target_pairs={{0,1},{1,2},{2,3},{3,4},{4,5},{5,6},{6,7},{7,8},{8,9},{9,10},{10,1... | collective-permute-start | bytes 393224 | tf_op jit(solution)/shard_map/ppermute | solution.py:18
  10.8 10.6 %collective-permute-start.1 = (bf16[1,512,128]{2,1,0:T(8,128)(2,1)S(1)}, bf16[1,512,128]{2,1,0:T(8,128)(2,1)S(1)}, u32[]{:S(2)}, u32[]{:S(2)}) collective-permute-start(bf16[1,512,128]{2,1,0:T(8,128)(2,1)S(1)} %get-tuple-element.79), channel_id=1, source_target_pairs={{1,0},{2,1},{3,2},{4,3},{5,4},{6,5},{7,6},{8,7},{9,8},{10,9},{11,1... | collective-permute-start | bytes 393224 | tf_op jit(solution)/shard_map/ppermute | solution.py:20
  24.7 10.9 %copy-start.7 = (bf16[3,3,128,128]{3,2,1,0:T(8,128)(2,1)S(1)}, bf16[3,3,128,128]{3,2,1,0:T(8,128)(2,1)}, u32[]{:S(2)}) copy-start(bf16[3,3,128,128]{3,2,1,0:T(8,128)(2,1)} %param.17) | copy-start | bytes 884740
  26.2 10.0 %collective-permute-start.2 = (bf16[1,512,128]{2,1,0:T(8,128)(2,1)S(1)}, bf16[1,512,128]{2,1,0:T(8,128)(2,1)S(1)}, u32[]{:S(2)}, u32[]{:S(2)}) collective-permute-start(bf16[1,512,128]{2,1,0:T(8,128)(2,1)S(1)} %get-tuple-element.76), channel_id=1, source_target_pairs={{0,1},{1,2},{2,3},{3,4},{4,5},{5,6},{6,7},{7,8},{8,9},{9,10},{10,1... | collective-permute-start | bytes 393224 | tf_op jit(solution)/shard_map/ppermute | solution.py:18
  28.2 9.9 %collective-permute-start.3 = (bf16[1,512,128]{2,1,0:T(8,128)(2,1)S(1)}, bf16[1,512,128]{2,1,0:T(8,128)(2,1)S(1)}, u32[]{:S(2)}, u32[]{:S(2)}) collective-permute-start(bf16[1,512,128]{2,1,0:T(8,128)(2,1)S(1)} %get-tuple-element.77), channel_id=1, source_target_pairs={{1,0},{2,1},{3,2},{4,3},{5,4},{6,5},{7,6},{8,7},{9,8},{10,9},{11,1... | collective-permute-start | bytes 393224 | tf_op jit(solution)/shard_map/ppermute | solution.py:20
  41.4 2.6 copy-start.13
  42.7 1.3 copy-start.2
  44.0 1.6 copy-start.11
  220.1 9.7 %copy-start.5 = (bf16[8,512,128]{2,1,0:T(8,128)(2,1)S(1)}, bf16[8,512,128]{2,1,0:T(8,128)(2,1)}, u32[]{:S(2)}) copy-start(bf16[8,512,128]{2,1,0:T(8,128)(2,1)} %multiply_convert_fusion) | copy-start | bytes 3145732
  220.1 9.7 %copy-start.9 = (bf16[128,128]{1,0:T(8,128)(2,1)S(1)}, bf16[128,128]{1,0:T(8,128)(2,1)}, u32[]{:S(2)}) copy-start(bf16[128,128]{1,0:T(8,128)(2,1)} %param.18) | copy-start | bytes 98308
  220.4 11.3 %collective-permute-start.4 = (bf16[2,1,512,128]{3,2,1,0:T(8,128)(2,1)S(1)}, bf16[2,1,512,128]{3,2,1,0:T(8,128)(2,1)S(1)}, u32[]{:S(2)}, u32[]{:S(2)}) collective-permute-start(bf16[2,1,512,128]{3,2,1,0:T(8,128)(2,1)S(1)} %get-tuple-element.74), channel_id=1, source_target_pairs={{0,1},{1,2},{2,3},{3,4},{4,5},{5,6},{6,7},{7,8},{8,9},{9,10},{10,1... | collective-permute-start | bytes 786440 | tf_op jit(solution)/shard_map/ppermute | solution.py:18
  222.3 11.1 %collective-permute-start.5 = (bf16[2,1,512,128]{3,2,1,0:T(8,128)(2,1)S(1)}, bf16[2,1,512,128]{3,2,1,0:T(8,128)(2,1)S(1)}, u32[]{:S(2)}, u32[]{:S(2)}) collective-permute-start(bf16[2,1,512,128]{3,2,1,0:T(8,128)(2,1)S(1)} %get-tuple-element.75), channel_id=1, source_target_pairs={{1,0},{2,1},{3,2},{4,3},{5,4},{6,5},{7,6},{8,7},{9,8},{10,9},{11,1... | collective-permute-start | bytes 786440 | tf_op jit(solution)/shard_map/ppermute | solution.py:20
  233.8 2.4 copy-start.10
  251.1 1.0 copy-start.4
  267.3 1.0 copy-start.4
  283.4 1.0 copy-start.4
  299.6 1.0 copy-start.4
  315.7 1.0 copy-start.4
  331.9 1.0 copy-start.4
  348.0 1.0 copy-start.4
  364.1 1.0 copy-start.4
  367.6 2.4 copy-start.3
  367.6 2.4 copy-start.12
  370.0 3.0 copy-start.1
Sparse Core Ops, SparseCore 0:
  45.7 169.9 all-gather.2
where the time goes:
time: 382 us; the launch traced here: 380 us
  waiting for transfers between devices  176 us (46%)
  matrix products  81.6 us (21%)
  local copies, waits for them, and re-layouts  32.7 us (9%)
  starting transfers between devices  28.6 us (7%)
  other arithmetic  25.3 us (7%)
  loops' own time  21.9 us (6%)
  between operations  13.7 us (4%)
    all_gather x1, waiting for transfers between devices, route_pair(): every_view = lax.all_gather(normed_rows[None], 'view', axis=0, tiled=True)  170 us
    dot_general x16, matrix products, attend_row(): jnp.dot(blended, out_weight, preferred_element_type=jnp.float32)  40.5 us
    dot_general x16, matrix products, attend_row(): lax.dot_general(query_row, key_window[partner], (((1,), (1,)), ((), ())),...  25.1 us
    ppermute x3, starting transfers between devices, extended(): lax.ppermute(head, axis, [((i + 1) % count, i) for i in range(ends)])  22.9 us
    another operation x1, loops' own time, per_device(): messages = lax.map(attend_row, jnp.arange(row_count, dtype=jnp.int32))  21.9 us
    slice x8, local copies, waits for them, and re-layouts, attend_row(): value_window[partner]  18.9 us
    dot_general x18, matrix products, convolve(): jnp.dot(window.reshape(-1, channels), kernel[row_tap, col_tap], preferred...  9.82 us
    reduce_sum x16, other arithmetic, attend_row(): jnp.sum(lifted, axis=-1, keepdims=True)  9.08 us
  transfers between devices with their start and end apart: 7, of which 6 were waited for; matrix products, arithmetic and copies ran while one was open for 1% of the time, Pallas kernels for 0%

commit v1 on v0

--- a/solution.py
+++ b/solution.py
@@ -49,7 +49,9 @@
 
 
 def route_pair(normed_rows, own_view, partners):
-    every_view = lax.all_gather(normed_rows[None], "view", axis=0, tiled=True)
+    own = normed_rows[None]
+    stack = jnp.stack([own] * lax.axis_size("view"))
+    every_view = jnp.concatenate(lax.all_to_all(stack, "view", 0, 0), axis=0)
     chosen = lax.dynamic_index_in_dim(partners, own_view, 0, keepdims=False)
     return jnp.take(every_view, chosen, axis=0)
 

time: 382 us -> 322 us (0.84)
  waiting for transfers between devices: 176 us -> 93.9 us
  local copies, waits for them, and re-layouts: 32.7 us -> 53.3 us
  between operations: 13.7 us -> 0.3 us
  starting transfers between devices: 28.6 us -> 35.8 us
  loops' own time: 21.9 us -> 27.1 us
    all_gather x1 -> x0, waiting for transfers between devices: 170 us -> none  [route_pair(): every_view = lax.all_gather(normed_rows[None], 'view', axis=0, tiled=True)]
    all_to_all x0 -> x1, waiting for transfers between devices: none -> 87.7 us  [route_pair(): every_view = jnp.concatenate(lax.all_to_all(stack, 'view', 0, 0), axis=0)]
    while x16 -> x32, local copies, waits for them, and re-layouts: 3.45 us -> 16.5 us
    all_to_all x0 -> x1, starting transfers between devices: none -> 6.02 us  [route_pair(): every_view = jnp.concatenate(lax.all_to_all(stack, 'view', 0, 0), axis=0)]
    another operation x0 -> x1, local copies, waits for them, and re-layouts: none -> 5.43 us  [route_pair(): stack = jnp.stack([own] * lax.axis_size('view'))]
    another operation x1, loops' own time: 21.9 us -> 27.1 us  [per_device(): messages = lax.map(attend_row, jnp.arange(row_count, dtype=jnp.int32))]
where the time goes in v1:
time: 322 us; the launch traced here: 320 us
  waiting for transfers between devices  93.9 us (29%)
  matrix products  84.8 us (26%)
  local copies, waits for them, and re-layouts  53.3 us (17%)
  starting transfers between devices  35.8 us (11%)
  loops' own time  27.1 us (8%)
  other arithmetic  24.5 us (8%)
    all_to_all x1, waiting for transfers between devices, route_pair(): every_view = jnp.concatenate(lax.all_to_all(stack, 'view', 0, 0), axis=0)  87.7 us
    dot_general x16, matrix products, attend_row(): jnp.dot(blended, out_weight, preferred_element_type=jnp.float32)  42.5 us
    another operation x1, loops' own time, per_device(): messages = lax.map(attend_row, jnp.arange(row_count, dtype=jnp.int32))  27.1 us
    dot_general x16, matrix products, attend_row(): lax.dot_general(query_row, key_window[partner], (((1,), (1,)), ((), ())),...  26.5 us
    ppermute x3, starting transfers between devices, extended(): lax.ppermute(head, axis, [((i + 1) % count, i) for i in range(ends)])  24 us
    slice x8, local copies, waits for them, and re-layouts, attend_row(): value_window[partner]  20.3 us
    while x32, local copies, waits for them, and re-layouts  16.5 us
    dot_general x18, matrix products, convolve(): jnp.dot(window.reshape(-1, channels), kernel[row_tap, col_tap], preferred...  9.67 us
  transfers between devices with their start and end apart: 7, of which 6 were waited for; matrix products, arithmetic and copies ran while one was open for 1% of the time, Pallas kernels for 0%

profile of v1, /device:TPU:6, one launch (start us, length us, event | category | flops | bytes accessed | tf_op | source)
XLA Modules:
  0.0 319.7 jit_solution(17188495679478864343)
XLA Ops:
  0.0 2.3 fusion.19
  2.3 1.9 collective-permute-start
  4.3 8.0 %collective-permute-start.1 = (bf16[1,512,128]{2,1,0:T(8,128)(2,1)S(1)}, bf16[1,512,128]{2,1,0:T(8,128)(2,1)S(1)}, u32[]{:S(2)}, u32[]{:S(2)}) collective-permute-start(bf16[1,512,128]{2,1,0:T(8,128)(2,1)S(1)} %get-tuple-element.79), channel_id=1, source_target_pairs={{1,0},{2,1},{3,2},{4,3},{5,4},{6,5},{7,6},{8,7},{9,8},{10,9},{11,1... | collective-permute-start | bytes 393224 | tf_op jit(solution)/shard_map/ppermute | solution.py:20
  13.0 1.8 collective-permute-done.1
  19.5 1.9 collective-permute-start.2
  21.5 7.4 %collective-permute-start.3 = (bf16[1,512,128]{2,1,0:T(8,128)(2,1)S(1)}, bf16[1,512,128]{2,1,0:T(8,128)(2,1)S(1)}, u32[]{:S(2)}, u32[]{:S(2)}) collective-permute-start(bf16[1,512,128]{2,1,0:T(8,128)(2,1)S(1)} %get-tuple-element.77), channel_id=1, source_target_pairs={{1,0},{2,1},{3,2},{4,3},{5,4},{6,5},{7,6},{8,7},{9,8},{10,9},{11,1... | collective-permute-start | bytes 393224 | tf_op jit(solution)/shard_map/ppermute | solution.py:20
  29.6 1.8 collective-permute-done.3
  38.1 5.4 %stack.3 = bf16[8,1,8,512,128]{4,3,2,1,0:T(8,128)(2,1)} broadcast(bf16[8,512,128]{2,1,0:T(8,128)(2,1)S(1)} %multiply_convert_fusion), dimensions={2,3,4} | broadcast | bytes 9437184 | tf_op jit(solution)/shard_map/stack | solution.py:53
  43.5 6.0 %all-to-all-start = ((bf16[8,1,8,512,128]{4,3,2,1,0:T(8,128)(2,1)}), bf16[8,1,8,512,128]{4,3,2,1,0:T(8,128)(2,1)}, u32[]{:S(2)}, u32[]{:S(2)}) async-start(bf16[8,1,8,512,128]{4,3,2,1,0:T(8,128)(2,1)} %stack.3), calls=%async_computation | async-start | bytes 16777216 | tf_op jit(solution)/shard_map/all_to_all | solution.py:54
  49.8 87.7 %all-to-all-done = bf16[8,1,8,512,128]{4,3,2,1,0:T(8,128)(2,1)} async-done(((bf16[8,1,8,512,128]{4,3,2,1,0:T(8,128)(2,1)}), bf16[8,1,8,512,128]{4,3,2,1,0:T(8,128)(2,1)}, u32[]{:S(2)}, u32[]{:S(2)}) %all-to-all-start) | async-done | bytes 8388640 | tf_op jit(solution)/shard_map/all_to_all | solution.py:54
  137.4 4.3 %gather_fusion = bf16[2,8,512,128]{3,2,1,0:T(8,128)(2,1)S(1)} fusion(bf16[8,8,512,128]{3,2,1,0:T(8,128)(2,1)} %bitcast.48, s32[1024]{0:T(1024)S(1)} %pad_clamp_fusion), kind=kCustom, calls=%fused_computation | custom fusion | bytes 4194312 | tf_op jit(solution)/shard_map/jit(_take)/gather | solution.py:56
  142.1 1.9 collective-permute-start.4
  144.0 8.5 %collective-permute-start.5 = (bf16[2,1,512,128]{3,2,1,0:T(8,128)(2,1)S(1)}, bf16[2,1,512,128]{3,2,1,0:T(8,128)(2,1)S(1)}, u32[]{:S(2)}, u32[]{:S(2)}) collective-permute-start(bf16[2,1,512,128]{3,2,1,0:T(8,128)(2,1)S(1)} %get-tuple-element.75), channel_id=1, source_target_pairs={{1,0},{2,1},{3,2},{4,3},{5,4},{6,5},{7,6},{8,7},{9,8},{10,9},{11,1... | collective-permute-start | bytes 786440 | tf_op jit(solution)/shard_map/ppermute | solution.py:20
  154.7 1.8 collective-permute-done.5
  156.8 2.3 convolution_convert_fusion.1
  159.1 2.3 convolution_convert_fusion
  161.5 152.9 %while.10 = (s32[]{:T(128)}, f32[8,512,128]{2,1,0:T(8,128)}, s32[8]{0:T(128)S(1)}, bf16[8,512,128]{2,1,0:T(8,128)(2,1)}, bf16[2,10,512,128]{3,2,1,0:T(8,128)(2,1...) while((s32[]{:T(128)}, f32[8,512,128]{2,1,0:T(8,128)}, ...), condition=%wide.region_6.7_spmd, body=%wide.region_1.0_spmd.sunk | while | flops 850065920 | bytes 38892316 | solution.py:135
  164.1 2.5 constant_dynamic-slice_fusion.5
  175.3 2.8 fusion.148
  178.0 2.5 fusion.151
  183.2 2.5 constant_dynamic-slice_fusion.5
  194.4 2.8 fusion.148
  197.1 2.5 fusion.151
  202.3 2.5 constant_dynamic-slice_fusion.5
  207.0 1.7 fusion.149
  213.5 2.8 fusion.148
  216.2 2.5 fusion.151
  221.5 2.5 constant_dynamic-slice_fusion.5
  226.1 1.7 fusion.149
  232.6 2.8 fusion.148
  235.3 2.5 fusion.151
  240.6 2.5 constant_dynamic-slice_fusion.5
  245.2 1.7 fusion.149
  251.7 2.8 fusion.148
  254.5 2.5 fusion.151
  259.7 2.5 constant_dynamic-slice_fusion.5
  264.3 1.7 fusion.149
  270.8 2.8 fusion.148
  273.6 2.5 fusion.151
  278.8 2.5 constant_dynamic-slice_fusion.5
  283.4 1.7 fusion.149
  289.9 2.8 fusion.148
  292.7 2.5 fusion.151
  297.9 2.5 constant_dynamic-slice_fusion.5
  309.0 2.8 fusion.148
  311.8 2.5 fusion.151
  314.3 2.4 multiply_reduce_fusion
  316.7 2.9 add_bitcast_fusion
  (139 shorter events, 70.0 us)
Async XLA Ops:
  0.0 156.8 %copy-start = (bf16[128,128]{1,0:T(8,128)(2,1)S(1)}, bf16[128,128]{1,0:T(8,128)(2,1)}, u32[]{:S(2)}) copy-start(bf16[128,128]{1,0:T(8,128)(2,1)} %param.19) | copy-start | bytes 98308
  0.0 12.3 %copy-start.6 = (f32[1,8,512,128]{3,2,1,0:T(8,128)S(1)}, f32[1,8,512,128]{3,2,1,0:T(8,128)}, u32[]{:S(2)}) copy-start(f32[1,8,512,128]{3,2,1,0:T(8,128)} %param.13) | copy-start | bytes 6291460
  0.0 12.3 %copy-start.8 = (bf16[3,3,128,128]{3,2,1,0:T(8,128)(2,1)S(1)}, bf16[3,3,128,128]{3,2,1,0:T(8,128)(2,1)}, u32[]{:S(2)}) copy-start(bf16[3,3,128,128]{3,2,1,0:T(8,128)(2,1)} %param.16) | copy-start | bytes 884740
  2.3 10.7 %collective-permute-start = (bf16[1,512,128]{2,1,0:T(8,128)(2,1)S(1)}, bf16[1,512,128]{2,1,0:T(8,128)(2,1)S(1)}, u32[]{:S(2)}, u32[]{:S(2)}) collective-permute-start(bf16[1,512,128]{2,1,0:T(8,128)(2,1)S(1)} %get-tuple-element.78), channel_id=1, source_target_pairs={{0,1},{1,2},{2,3},{3,4},{4,5},{5,6},{6,7},{7,8},{8,9},{9,10},{10,1... | collective-permute-start | bytes 393224 | tf_op jit(solution)/shard_map/ppermute | solution.py:18
  4.3 10.6 %collective-permute-start.1 = (bf16[1,512,128]{2,1,0:T(8,128)(2,1)S(1)}, bf16[1,512,128]{2,1,0:T(8,128)(2,1)S(1)}, u32[]{:S(2)}, u32[]{:S(2)}) collective-permute-start(bf16[1,512,128]{2,1,0:T(8,128)(2,1)S(1)} %get-tuple-element.79), channel_id=1, source_target_pairs={{1,0},{2,1},{3,2},{4,3},{5,4},{6,5},{7,6},{8,7},{9,8},{10,9},{11,1... | collective-permute-start | bytes 393224 | tf_op jit(solution)/shard_map/ppermute | solution.py:20
  18.1 10.8 %copy-start.7 = (bf16[3,3,128,128]{3,2,1,0:T(8,128)(2,1)S(1)}, bf16[3,3,128,128]{3,2,1,0:T(8,128)(2,1)}, u32[]{:S(2)}) copy-start(bf16[3,3,128,128]{3,2,1,0:T(8,128)(2,1)} %param.17) | copy-start | bytes 884740
  19.5 10.1 %collective-permute-start.2 = (bf16[1,512,128]{2,1,0:T(8,128)(2,1)S(1)}, bf16[1,512,128]{2,1,0:T(8,128)(2,1)S(1)}, u32[]{:S(2)}, u32[]{:S(2)}) collective-permute-start(bf16[1,512,128]{2,1,0:T(8,128)(2,1)S(1)} %get-tuple-element.76), channel_id=1, source_target_pairs={{0,1},{1,2},{2,3},{3,4},{4,5},{5,6},{6,7},{7,8},{8,9},{9,10},{10,1... | collective-permute-start | bytes 393224 | tf_op jit(solution)/shard_map/ppermute | solution.py:18
  21.5 9.9 %collective-permute-start.3 = (bf16[1,512,128]{2,1,0:T(8,128)(2,1)S(1)}, bf16[1,512,128]{2,1,0:T(8,128)(2,1)S(1)}, u32[]{:S(2)}, u32[]{:S(2)}) collective-permute-start(bf16[1,512,128]{2,1,0:T(8,128)(2,1)S(1)} %get-tuple-element.77), channel_id=1, source_target_pairs={{1,0},{2,1},{3,2},{4,3},{5,4},{6,5},{7,6},{8,7},{9,8},{10,9},{11,1... | collective-permute-start | bytes 393224 | tf_op jit(solution)/shard_map/ppermute | solution.py:20
  34.7 2.6 copy-start.13
  36.0 1.3 copy-start.4
  43.5 6.0 %copy-start.11 = (s32[8,2]{0,1:T(2,128)S(1)}, s32[8,2]{0,1:T(2,128)}, u32[]{:S(2)}) copy-start(s32[8,2]{0,1:T(2,128)} %param.15) | copy-start | bytes 196
  43.5 93.9 %all-to-all-start = ((bf16[8,1,8,512,128]{4,3,2,1,0:T(8,128)(2,1)}), bf16[8,1,8,512,128]{4,3,2,1,0:T(8,128)(2,1)}, u32[]{:S(2)}, u32[]{:S(2)}) async-start(bf16[8,1,8,512,128]{4,3,2,1,0:T(8,128)(2,1)} %stack.3), calls=%async_computation | async-start | bytes 16777216 | tf_op jit(solution)/shard_map/all_to_all | solution.py:54
  141.8 10.8 %copy-start.9 = (bf16[128,128]{1,0:T(8,128)(2,1)S(1)}, bf16[128,128]{1,0:T(8,128)(2,1)}, u32[]{:S(2)}) copy-start(bf16[128,128]{1,0:T(8,128)(2,1)} %param.18) | copy-start | bytes 98308
  142.1 12.6 %collective-permute-start.4 = (bf16[2,1,512,128]{3,2,1,0:T(8,128)(2,1)S(1)}, bf16[2,1,512,128]{3,2,1,0:T(8,128)(2,1)S(1)}, u32[]{:S(2)}, u32[]{:S(2)}) collective-permute-start(bf16[2,1,512,128]{3,2,1,0:T(8,128)(2,1)S(1)} %get-tuple-element.74), channel_id=1, source_target_pairs={{0,1},{1,2},{2,3},{3,4},{4,5},{5,6},{6,7},{7,8},{8,9},{9,10},{10,1... | collective-permute-start | bytes 786440 | tf_op jit(solution)/shard_map/ppermute | solution.py:18
  144.0 12.4 %collective-permute-start.5 = (bf16[2,1,512,128]{3,2,1,0:T(8,128)(2,1)S(1)}, bf16[2,1,512,128]{3,2,1,0:T(8,128)(2,1)S(1)}, u32[]{:S(2)}, u32[]{:S(2)}) collective-permute-start(bf16[2,1,512,128]{3,2,1,0:T(8,128)(2,1)S(1)} %get-tuple-element.75), channel_id=1, source_target_pairs={{1,0},{2,1},{3,2},{4,3},{5,4},{6,5},{7,6},{8,7},{9,8},{10,9},{11,1... | collective-permute-start | bytes 786440 | tf_op jit(solution)/shard_map/ppermute | solution.py:20
  156.8 2.4 copy-start.10
  159.1 2.3 copy-start.14
  170.5 1.0 copy-start.3
  173.1 1.6 copy-start.2
  189.6 1.0 copy-start.3
  192.2 1.6 copy-start.2
  208.7 1.0 copy-start.3
  211.3 1.6 copy-start.2
  227.8 1.0 copy-start.3
  230.4 1.6 copy-start.2
  246.9 1.0 copy-start.3
  249.5 1.6 copy-start.2
  266.0 1.0 copy-start.3
  268.6 1.6 copy-start.2
  285.1 1.0 copy-start.3
  287.7 1.6 copy-start.2
  304.2 1.0 copy-start.3
  306.8 1.6 copy-start.2
  314.3 2.4 copy-start.5
  314.3 2.4 copy-start.12
  316.7 3.0 copy-start.1
